TPU v7x, 32 devices: a whole 2x2x4 slice. The times are simulated.
32 devices in a mesh: island: 4 (over x, core), fsdp: 8 (over z, y).
Axes of the slice: x: 2, y: 2, z: 4, core: 2. Of those that a mesh axis runs over, the one named last changes fastest.
Arguments:
- local_weights: bfloat16 [4, 64, 8192], P('island', 'fsdp'), may hold values from -6 to 6
- base_master: float32 [64, 8192], P('fsdp'), may hold values from -6 to 6
- momentum: float32 [64, 8192], P('fsdp'), may hold values from -4 to 4
Outputs:
- new_master: float32 [64, 8192], P('fsdp')
- new_momentum: float32 [64, 8192], P('fsdp')
- new_base: bfloat16 [64, 8192], replicated
All inputs are finite; a program needn't handle non-finite values.
Results may differ from a plain program's by a relative error of at most 0.02.
Values may be sent and summed in bfloat16 or wider, within the bound.
A program may use at most 64 MiB of HBM per device.

v0:
```python
import jax
import jax.numpy as jnp
from jax import lax
from jax.sharding import PartitionSpec as P

BLOCK = 128


epsilon = 1e-06
code_limit = 31.0
momentum_decay = 0.9
outer_rate = 0.7


def encode(outer_grad):
    blocks = outer_grad.reshape(outer_grad.shape[0], outer_grad.shape[1] // BLOCK, BLOCK)
    largest = jnp.max(jnp.abs(blocks), axis=2)
    block_scale = (largest + epsilon) / code_limit
    code_values = (blocks / block_scale[:, :, None]).astype(jnp.bfloat16)
    return (code_values, block_scale)


def outer_step(summed, base_rows, moment_rows, groups):
    averaged = summed / groups
    fresh_moment = momentum_decay * moment_rows + averaged
    fresh_master = base_rows - outer_rate * (averaged + momentum_decay * fresh_moment)
    return (fresh_master, fresh_moment)


def on_device(local_weights, base_master, momentum):
    groups = lax.axis_size("island")
    outer_grad = base_master - local_weights[0].astype(jnp.float32)
    code_values, block_scale = encode(outer_grad)
    all_codes, all_scales = (
        lax.all_gather(code_values[None], "island", axis=0, tiled=True),
        lax.all_gather(block_scale[None].astype(jnp.bfloat16), "island", axis=0, tiled=True).astype(
            jnp.float32
        ),
    )
    terms = all_codes.astype(jnp.float32) * all_scales[:, :, :, None]
    summed = jnp.sum(terms, axis=0).reshape(base_master.shape)
    new_master, new_momentum = outer_step(summed, base_master, momentum, groups)
    new_base = lax.all_gather(new_master.astype(jnp.bfloat16), "fsdp", axis=0, tiled=True)
    return (new_master, new_momentum, new_base)


def solution(mesh):
    return jax.shard_map(
        on_device,
        mesh=mesh,
        in_specs=(P("island", "fsdp", None), P("fsdp", None), P("fsdp", None)),
        out_specs=(P("fsdp", None), P("fsdp", None), P()),
        check_vma=False,
    )
```

profile of v0, /device:TPU:0, one launch (start us, length us, event | category | flops | bytes accessed | tf_op | source)
XLA Modules:
  0.0 75.8 jit_solution(18348891017853198195)
XLA Ops:
  7.2 0.0 copy-start
  7.2 0.0 copy-start.1
  7.2 0.0 all-gather.3.cloned.1.call-start
  7.2 1.2 %bitcast_reduce_fusion = f32[8,64]{0,1:T(8,128)S(1)} fusion(f32[8,8192]{1,0:T(8,128)} %param.4, bf16[1,8,8192]{2,1,0:T(8,128)(2,1)} %param.3), kind=kLoop, calls=%fused_computation.8 | loop fusion | flops 261632 | bytes 395264 | tf_op jit(solution)/shard_map/reduce_max | solution.py:17
  8.4 0.0 copy-done
  8.4 0.0 copy-done.1
  8.5 0.1 copy.12
  8.5 6.2 %all-gather = bf16[32,64]{1,0:T(8,128)(2,1)S(1)} all-gather(bf16[8,64]{1,0:T(8,128)(2,1)S(1)} %get-tuple-element.6), channel_id=2, replica_groups=mesh['island'=4,'fsdp'=8] {'island'}, dimensions={0}, use_global_device_ids=true | all-gather | bytes 5120 | tf_op jit(solution)/shard_map/all_gather | solution.py:36
  14.7 0.1 fusion.2
  14.9 7.7 %all_gather.9 = bf16[4,8,64,128]{3,2,1,0:T(8,128)(2,1)S(1)} all-gather(bf16[1,8,64,128]{3,2,1,0:T(8,128)(2,1)S(1)} %fusion.2), channel_id=1, replica_groups=mesh['island'=4,'fsdp'=8] {'island'}, dimensions={0}, use_global_device_ids=true | all-gather | bytes 655360 | tf_op jit(solution)/shard_map/all_gather | solution.py:35
  22.5 0.3 multiply_reduce_fusion
  22.9 0.0 copy-start.2
  22.9 0.9 %copy-done.2 = f32[8,8192]{1,0:T(8,128)S(1)} copy-done((f32[8,8192]{1,0:T(8,128)S(1)}, f32[8,8192]{1,0:T(8,128)}, u32[]{:S(2)}) %copy-start.2) | copy-done | bytes 262168
  23.8 1.0 %fusion.5 = (bf16[8,8192]{1,0:T(8,128)(2,1)}, f32[8,8192]{1,0:T(8,128)}, f32[8,8192]{1,0:T(8,128)}) fusion(f32[8,8192]{1,0:T(8,128)S(1)} %copy-done, f32[1,8,64,128]{3,2,1,0:T(8,128)S(1)} %multiply_bitcast_fusion, f32[8,8192]{1,0:T(8,128)S(1)} %copy-done.2), kind=kLoop, calls=%fused_computation.14 | loop fusion | flops 458752 | bytes 1441792 | tf_op jit(solution)/shard_map/convert_element_type | solution.py:43
  24.9 0.0 all-gather.3.cloned.1.call-update
  24.9 41.8 %all-gather.3.cloned.1.call-done = bf16[64,8192]{1,0:T(8,128)(2,1)} async-done(((bf16[8,8192]{1,0:T(8,128)(2,1)}), bf16[64,8192]{1,0:T(8,128)(2,1)}) %all-gather.3.cloned.1.call-update) | async-done | bytes 1048592 | tf_op jit(solution)/shard_map/all_gather | solution.py:43
  66.7 2.3 %copy.21 = bf16[64,8192]{1,0:T(8,128)(2,1)} copy(bf16[64,8192]{1,0:T(8,128)(2,1)} %all-gather.3.cloned.1.call-done) | data formatting | bytes 2097152
  (4 shorter events, 0.1 us)
Async XLA Ops:
  7.2 1.3 %copy-start = (f32[8,8192]{1,0:T(8,128)S(1)}, f32[8,8192]{1,0:T(8,128)}, u32[]{:S(2)}) copy-start(f32[8,8192]{1,0:T(8,128)} %param.4) | copy-start | bytes 786436
  7.2 1.3 %copy-start.1 = (bf16[1,8,8192]{2,1,0:T(8,128)(2,1)S(1)}, bf16[1,8,8192]{2,1,0:T(8,128)(2,1)}, u32[]{:S(2)}) copy-start(bf16[1,8,8192]{2,1,0:T(8,128)(2,1)} %param.3) | copy-start | bytes 393220
  7.2 59.5 %all-gather.3.cloned.1.call-start = ((), (), s32[]{:S(2)}) async-start(), calls=%async_computation | async-start | bytes 1179648 | tf_op jit(solution)/shard_map/all_gather | solution.py:43
  22.9 1.0 %copy-start.2 = (f32[8,8192]{1,0:T(8,128)S(1)}, f32[8,8192]{1,0:T(8,128)}, u32[]{:S(2)}) copy-start(f32[8,8192]{1,0:T(8,128)} %param.5) | copy-start | bytes 786436
Sparse Core Ops, SparseCore 0:
  25.0 41.6 all-gather.2
where the time goes:
time: 76 us; the launch traced here: 75.8 us
  waiting for transfers between devices  41.8 us (55%)
  between operations  14.1 us (19%)
  blocking collectives  13.8 us (18%)
  local copies, waits for them, and re-layouts  3.25 us (4%)
  other arithmetic  2.75 us (4%)
    all_gather x1, waiting for transfers between devices, on_device(): lax.all_gather(new_master.astype(jnp.bfloat16), 'fsdp', axis=0, tiled=True)  41.8 us
    all_gather x1, blocking collectives, on_device(): lax.all_gather(code_values[None], 'island', axis=0, tiled=True)  7.67 us
    all_gather x1, blocking collectives, on_device(): lax.all_gather(block_scale[None].astype(jnp.bfloat16), 'island', axis=0,...  6.16 us
    unnamed x7, local copies, waits for them, and re-layouts  3.19 us
  transfers between devices with their start and end apart: 1, of which 1 were waited for; matrix products, arithmetic and copies ran while one was open for 0% of the time, Pallas kernels for 0%

commit v1 on v0

v1 whole, which is shorter than its diff:
```python
import functools

import jax
import jax.numpy as jnp
from jax import lax
from jax.experimental import pallas as pl
from jax.experimental.pallas import tpu as pltpu
from jax.sharding import PartitionSpec as P

BLOCK = 128
CHUNKS = 2
UNROLL = 8

epsilon = 1e-06
code_limit = 31.0
momentum_decay = 0.9
outer_rate = 0.7


def flip(index, mask):
    out = index
    bit = 1
    while bit <= mask:
        if mask & bit:
            out = out + bit - 2 * bit * lax.rem(lax.div(index, bit), 2)
        bit *= 2
    return out


def decoded(outer_grad):
    largest = jnp.max(jnp.abs(outer_grad), axis=1, keepdims=True)
    block_scale = (largest + epsilon) / code_limit
    coded = (outer_grad / block_scale).astype(jnp.bfloat16)
    return coded.astype(jnp.float32) * block_scale


def kernel(
    groups,
    n,
    weights_in,
    base_in,
    moment_in,
    master_out,
    moment_out,
    rows_out,
    weights,
    base,
    moment,
    load_sem,
    island_send,
    island_recv,
    line_send,
    pair_send,
    core_send,
    rows_recv,
):
    isl = lax.axis_index("island")
    shard = lax.axis_index("fsdp")
    mine = lax.rem(isl, 2)
    width = base.shape[1]
    half = width // 2
    piece = half // CHUNKS
    lines = range(2, n, 2)

    loads = [
        pltpu.make_async_copy(weights_in.at[0], weights.at[isl], load_sem.at[0]),
        pltpu.make_async_copy(base_in, base, load_sem.at[1]),
        pltpu.make_async_copy(moment_in, moment, load_sem.at[2]),
    ]
    for load in loads:
        load.start()

    barrier = pltpu.get_barrier_semaphore()
    partners = [(flip(isl, m), shard) for m in range(1, groups)]
    partners += [(isl, flip(shard, m)) for m in (1, *lines)]
    for partner in partners:
        pl.semaphore_signal(barrier, inc=1, device_id=partner, device_id_type=pl.DeviceIdType.MESH)
    loads[0].wait()
    pl.semaphore_wait(barrier, len(partners))

    def columns(side, k):
        return pl.ds(pl.multiple_of(side * half + k * piece, BLOCK), piece)

    def remote(ref, send, recv, partner):
        return pltpu.make_async_remote_copy(
            src_ref=ref,
            dst_ref=ref,
            send_sem=send,
            recv_sem=recv,
            device_id=partner,
            device_id_type=pl.DeviceIdType.MESH,
        )

    sent = []

    def send(copy):
        copy.start()
        sent.append(copy)

    def island_copy(source, side, k, mask, send_at, recv_at):
        return remote(
            weights.at[source, :, columns(side, k)],
            island_send.at[send_at],
            island_recv.at[recv_at],
            (flip(isl, mask), shard),
        )

    def rows_copy(mask, side, k, send_sem, recv_at, partner):
        return remote(
            rows_out.at[flip(shard, mask), :, columns(side, k)],
            send_sem,
            rows_recv.at[recv_at],
            partner,
        )

    for k in range(CHUNKS):
        for m in range(2, groups):
            side = mine if m % 2 == 0 else 1 - mine
            send(island_copy(isl, side, k, m, (m, 0, k), (m, 0, k)))
        send(island_copy(isl, 1 - mine, k, 1, (1, 0, k), (1, 0, k)))
    for k in range(CHUNKS):
        send(island_copy(isl, mine, k, 1, (1, 1, k), (1, 1, k)))
    loads[1].wait()
    loads[2].wait()

    def update(side, k):
        start = side * half + k * piece

        def step(t, carry):
            for u in range(UNROLL):
                at = pl.ds(pl.multiple_of(start + (t * UNROLL + u) * BLOCK, BLOCK), BLOCK)
                held = base[:, at]
                summed = None
                for m in range(groups):
                    term = decoded(held - weights[flip(isl, m), :, at].astype(jnp.float32))
                    summed = term if summed is None else summed + term
                averaged = summed / groups
                fresh_moment = momentum_decay * moment[:, at] + averaged
                fresh_master = held - outer_rate * (averaged + momentum_decay * fresh_moment)
                moment_out[:, at] = fresh_moment
                master_out[:, at] = fresh_master
                rows_out[shard, :, at] = fresh_master.astype(jnp.bfloat16)
            return carry

        lax.fori_loop(0, piece // (BLOCK * UNROLL), step, 0)

    def wait_island(mask, rel, k):
        island_copy(
            flip(isl, mask), mine if rel == 0 else 1 - mine, k, 1, (mask, rel, k), (mask, rel, k)
        ).wait_recv()

    def wait_rows(mask, rel, k):
        rows_copy(
            mask, mine if rel == 0 else 1 - mine, k, core_send.at[mask, k], (mask, rel, k), (flip(isl, 1), shard)
        ).wait_recv()

    pair = (isl, flip(shard, 1))
    core = (flip(isl, 1), shard)

    for k in range(CHUNKS):
        for m in range(1, groups):
            wait_island(m, 0, k)
            if m > 1:
                send(island_copy(flip(isl, m), mine, k, 1, (m, 1, k), (m ^ 1, 1, k)))
        update(mine, k)
        for m in lines:
            send(rows_copy(0, mine, k, line_send.at[m // 2, k], (m, 0, k), (isl, flip(shard, m))))
        send(rows_copy(0, mine, k, pair_send.at[0, k], (1, 0, k), pair))

    for k in range(CHUNKS):
        for m in range(1, groups):
            wait_island(m, 1, k)
        update(1 - mine, k)

    for k in range(CHUNKS):
        wait_rows(1, 0, k)
        send(rows_copy(1, mine, k, core_send.at[1, k], (1, 1, k), core))
        for m in lines:
            wait_rows(m, 0, k)
            send(rows_copy(m, mine, k, pair_send.at[m // 2, k], (m + 1, 0, k), pair))
            send(rows_copy(m, mine, k, core_send.at[m, k], (m, 1, k), core))
    for k in range(CHUNKS):
        for m in lines:
            wait_rows(m + 1, 0, k)
            send(rows_copy(m + 1, mine, k, core_send.at[m + 1, k], (m + 1, 1, k), core))
    for k in range(CHUNKS):
        for m in range(1, n):
            wait_rows(m, 1, k)
    for copy in sent:
        copy.wait_send()


def solution(mesh):
    groups, n = mesh.shape["island"], mesh.shape["fsdp"]

    def on_device(local_weights, base_master, momentum):
        rows, width = base_master.shape
        vmem = pl.BlockSpec(memory_space=pltpu.VMEM)
        hbm = pl.BlockSpec(memory_space=pltpu.HBM)
        new_master, new_momentum, all_rows = pl.pallas_call(
            functools.partial(kernel, groups, n),
            out_shape=(
                jax.ShapeDtypeStruct((rows, width), jnp.float32),
                jax.ShapeDtypeStruct((rows, width), jnp.float32),
                jax.ShapeDtypeStruct((n, rows, width), jnp.bfloat16),
            ),
            in_specs=[hbm] * 3,
            out_specs=(vmem,) * 3,
            scratch_shapes=[
                pltpu.VMEM((groups, rows, width), jnp.bfloat16),
                pltpu.VMEM((rows, width), jnp.float32),
                pltpu.VMEM((rows, width), jnp.float32),
                pltpu.SemaphoreType.DMA((3,)),
                pltpu.SemaphoreType.DMA((groups, 2, CHUNKS)),
                pltpu.SemaphoreType.DMA((groups, 2, CHUNKS)),
                pltpu.SemaphoreType.DMA((n // 2, CHUNKS)),
                pltpu.SemaphoreType.DMA((n // 2, CHUNKS)),
                pltpu.SemaphoreType.DMA((n, CHUNKS)),
                pltpu.SemaphoreType.DMA((n, 2, CHUNKS)),
            ],
            compiler_params=pltpu.CompilerParams(collective_id=0, has_side_effects=True),
        )(local_weights, base_master, momentum)
        return new_master, new_momentum, all_rows.reshape(n * rows, width)

    return jax.shard_map(
        on_device,
        mesh=mesh,
        in_specs=(P("island", "fsdp", None), P("fsdp", None), P("fsdp", None)),
        out_specs=(P("fsdp", None), P("fsdp", None), P()),
        check_vma=False,
    )
```

time: 76 us -> 27.8 us (0.37)
  waiting for transfers between devices: 41.8 us -> 0 us
  Pallas kernels: 0 us -> 22.6 us
  blocking collectives: 13.8 us -> 0 us
  between operations: 14.1 us -> 0.65 us
  other arithmetic: 2.75 us -> 0 us
  local copies, waits for them, and re-layouts: 3.25 us -> 4.4 us
    all_gather x1 -> x0, waiting for transfers between devices: 41.8 us -> none  [on_device(): lax.all_gather(new_master.astype(jnp.bfloat16), 'fsdp', axis=0, tiled=True)]
    pallas_call x0 -> x1, Pallas kernels: none -> 22.6 us  [on_device(): pl.pallas_call(functools.partial(kernel, groups, n), out_shape=(jax.Shape...]
    all_gather x2 -> x0, blocking collectives: 13.8 us -> none  [the longest x1 7.67 us: on_device(): lax.all_gather(code_values[None], 'island', axis=0, tiled=True)]
    unnamed x7 -> x5, local copies, waits for them, and re-layouts: 3.19 us -> 4.4 us
    convert_element_type x4 -> x0, other arithmetic: 1.19 us -> none  [the longest x1 1.04 us: on_device(): new_master.astype(jnp.bfloat16)]
    reduce_max x1 -> x0, other arithmetic: 1.18 us -> none  [encode(): largest = jnp.max(jnp.abs(blocks), axis=2)]
  transfers between devices with their start and end apart: 1 -> 0, of which waited for: 1 -> 0; matrix products, arithmetic and copies ran while one was open for 0% -> 0% of each run, Pallas kernels for 0% -> 0%
where the time goes in v1:
time: 27.8 us; the launch traced here: 27.6 us
  Pallas kernels  22.6 us (81%)
  local copies, waits for them, and re-layouts  4.4 us (16%)
  between operations  0.65 us (2%)
    pallas_call x1, Pallas kernels, on_device(): pl.pallas_call(functools.partial(kernel, groups, n), out_shape=(jax.Shape...  22.6 us
    unnamed x5, local copies, waits for them, and re-layouts  4.4 us

profile of v1, /device:TPU:0, one launch (start us, length us, event | category | flops | bytes accessed | tf_op | source)
XLA Modules:
  0.0 27.6 jit_solution(7360020084944702695)
XLA Ops:
  0.6 22.6 %shard_map.58 = (f32[8,8192]{1,0:T(8,128)}, f32[8,8192]{1,0:T(8,128)}, bf16[8,8,8192]{2,1,0:T(8,128)(2,1)}) custom-call(bf16[1,8,8192]{2,1,0:T(8,128)(2,1)} %weights_in.1, f32[8,8192]{1,0:T(8,128)} %base_in.1, f32[8,8192]{1,0:T(8,128)} %moment_in.1), custom_call_target="tpu_custom_call" | custom-call | tf_op jit(solution)/shard_map/pallas_call | solution.py:200
  23.2 0.0 copy-start
  23.2 1.8 %copy.9 = f32[8,8192]{1,0:T(8,128)} copy(f32[8,8192]{1,0:T(8,128)} %get-tuple-element.12) | data formatting | bytes 524288
  25.0 1.7 %copy.10 = f32[8,8192]{1,0:T(8,128)} copy(f32[8,8192]{1,0:T(8,128)} %get-tuple-element.13) | data formatting | bytes 524288
  26.7 0.0 copy-done
  26.7 1.0 %copy.11 = bf16[64,8192]{1,0:T(8,128)(2,1)} copy(bf16[64,8192]{1,0:T(8,128)(2,1)S(1)} %bitcast.1) | data formatting | bytes 2097152
Async XLA Ops:
  23.2 3.4 %copy-start = (bf16[8,8,8192]{2,1,0:T(8,128)(2,1)S(1)}, bf16[8,8,8192]{2,1,0:T(8,128)(2,1)}, u32[]{:S(2)}) copy-start(bf16[8,8,8192]{2,1,0:T(8,128)(2,1)} %get-tuple-element.8) | copy-start | bytes 3145732

commit v2 on v1

--- a/solution.py
+++ b/solution.py
@@ -190,6 +190,18 @@
         copy.wait_send()
 
 
+def store(master, moment, rows, master_out, moment_out, rows_out, sems):
+    copies = [
+        pltpu.make_async_copy(rows, rows_out, sems.at[0]),
+        pltpu.make_async_copy(master, master_out, sems.at[1]),
+        pltpu.make_async_copy(moment, moment_out, sems.at[2]),
+    ]
+    for copy in copies:
+        copy.start()
+    for copy in copies:
+        copy.wait()
+
+
 def solution(mesh):
     groups, n = mesh.shape["island"], mesh.shape["fsdp"]
 
@@ -200,9 +212,9 @@
         new_master, new_momentum, all_rows = pl.pallas_call(
             functools.partial(kernel, groups, n),
             out_shape=(
-                jax.ShapeDtypeStruct((rows, width), jnp.float32),
-                jax.ShapeDtypeStruct((rows, width), jnp.float32),
-                jax.ShapeDtypeStruct((n, rows, width), jnp.bfloat16),
+                pltpu.VMEM((rows, width), jnp.float32),
+                pltpu.VMEM((rows, width), jnp.float32),
+                pltpu.VMEM((n, rows, width), jnp.bfloat16),
             ),
             in_specs=[hbm] * 3,
             out_specs=(vmem,) * 3,
@@ -218,8 +230,20 @@
                 pltpu.SemaphoreType.DMA((n, CHUNKS)),
                 pltpu.SemaphoreType.DMA((n, 2, CHUNKS)),
             ],
-            compiler_params=pltpu.CompilerParams(collective_id=0, has_side_effects=True),
+            compiler_params=pltpu.CompilerParams(
+                collective_id=0, has_side_effects=True, vmem_limit_bytes=16 * 2**20
+            ),
         )(local_weights, base_master, momentum)
+        new_master, new_momentum, all_rows = pl.pallas_call(
+            store,
+            out_shape=tuple(
+                pltpu.HBM(x.shape, x.dtype) for x in (new_master, new_momentum, all_rows)
+            ),
+            in_specs=[vmem] * 3,
+            out_specs=(hbm,) * 3,
+            scratch_shapes=[pltpu.SemaphoreType.DMA((3,))],
+            compiler_params=pltpu.CompilerParams(vmem_limit_bytes=16 * 2**20),
+        )(*(pltpu.with_memory_space_constraint(x, pltpu.VMEM) for x in (new_master, new_momentum, all_rows)))
         return new_master, new_momentum, all_rows.reshape(n * rows, width)
 
     return jax.shard_map(

time: 27.8 us -> 26.4 us (0.950)
  local copies, waits for them, and re-layouts: 4.4 us -> 2.8 us
    unnamed x5 -> x6, local copies, waits for them, and re-layouts: 4.4 us -> 2.8 us
    pallas_call x1 -> x2, Pallas kernels: 22.6 us -> 22.7 us  [the longest x1 21.6 us: on_device(): pl.pallas_call(functools.partial(kernel, groups, n), out_shape=(pltpu.VME...]
where the time goes in v2:
time: 26.4 us; the launch traced here: 26.2 us
  Pallas kernels  22.7 us (86%)
  local copies, waits for them, and re-layouts  2.8 us (11%)
  between operations  0.65 us (2%)
    pallas_call x1, Pallas kernels, on_device(): pl.pallas_call(functools.partial(kernel, groups, n), out_shape=(pltpu.VME...  21.6 us
    unnamed x6, local copies, waits for them, and re-layouts  2.8 us
    pallas_call x1, Pallas kernels, on_device(): pl.pallas_call(store, out_shape=tuple((pltpu.HBM(x.shape, x.dtype) for x...  1.16 us

profile of v2, /device:TPU:0, one launch (start us, length us, event | category | flops | bytes accessed | tf_op | source)
XLA Modules:
  0.0 26.2 jit_solution(16628933089017516765)
XLA Ops:
  0.6 0.0 copy-start
  0.6 0.9 %copy-done = f32[8,8192]{1,0:T(8,128)S(1)} copy-done((f32[8,8192]{1,0:T(8,128)S(1)}, f32[8,8192]{1,0:T(8,128)}, u32[]{:S(2)}) %copy-start) | copy-done | bytes 262168
  1.6 0.0 copy-start.1
  1.6 0.9 %copy-done.1 = f32[8,8192]{1,0:T(8,128)S(1)} copy-done((f32[8,8192]{1,0:T(8,128)S(1)}, f32[8,8192]{1,0:T(8,128)}, u32[]{:S(2)}) %copy-start.1) | copy-done | bytes 262168
  2.5 0.0 copy-start.2
  2.5 0.9 %copy-done.2 = bf16[1,8,8192]{2,1,0:T(8,128)(2,1)S(1)} copy-done((bf16[1,8,8192]{2,1,0:T(8,128)(2,1)S(1)}, bf16[1,8,8192]{2,1,0:T(8,128)(2,1)}, u32[]{:S(2)}) %copy-start.2) | copy-done | bytes 131096
  3.4 21.6 %shard_map.58 = (f32[8,8192]{1,0:T(8,128)S(1)}, f32[8,8192]{1,0:T(8,128)S(1)}, bf16[8,8,8192]{2,1,0:T(8,128)(2,1)S(1)}) custom-call(bf16[1,8,8192]{2,1,0:T(8,128)(2,1)S(1)} %copy-done.2, f32[8,8192]{1,0:T(8,128)S(1)} %copy-done, f32[8,8192]{1,0:T(8,128)S(1)} %copy-done.1), custom_call_target="tpu_custom_call" | custom-call | tf_op jit(solution)/shard_map/pallas_call | solution.py:212
  25.0 1.2 %shard_map.59 = (f32[8,8192]{1,0:T(8,128)}, f32[8,8192]{1,0:T(8,128)}, bf16[8,8,8192]{2,1,0:T(8,128)(2,1)}) custom-call(f32[8,8192]{1,0:T(8,128)S(1)} %get-tuple-element.9.master, f32[8,8192]{1,0:T(8,128)S(1)} %get-tuple-element.10.moment, bf16[8,8,8192]{2,1,0:T(8,128)(2,1)S(1)} %get-tuple-element.11.rows), custom_call_target="tpu_custom_call" | custom-call | tf_op jit(solution)/shard_map/pallas_call | solution.py:237
Async XLA Ops:
  0.6 1.0 %copy-start = (f32[8,8192]{1,0:T(8,128)S(1)}, f32[8,8192]{1,0:T(8,128)}, u32[]{:S(2)}) copy-start(f32[8,8192]{1,0:T(8,128)} %base_in.1) | copy-start | bytes 786436
  1.6 0.9 %copy-start.1 = (f32[8,8192]{1,0:T(8,128)S(1)}, f32[8,8192]{1,0:T(8,128)}, u32[]{:S(2)}) copy-start(f32[8,8192]{1,0:T(8,128)} %moment_in.1) | copy-start | bytes 786436
  2.5 0.9 %copy-start.2 = (bf16[1,8,8192]{2,1,0:T(8,128)(2,1)S(1)}, bf16[1,8,8192]{2,1,0:T(8,128)(2,1)}, u32[]{:S(2)}) copy-start(bf16[1,8,8192]{2,1,0:T(8,128)(2,1)} %weights_in.1) | copy-start | bytes 393220

commit v3 on v2

--- a/solution.py
+++ b/solution.py
@@ -8,6 +8,8 @@
 from jax.sharding import PartitionSpec as P
 
 BLOCK = 128
+VMEM = 65472 * 2**10
+GRANT = 60 * 1024 * 2**10
 CHUNKS = 2
 UNROLL = 8
 
@@ -207,6 +209,8 @@
 
     def on_device(local_weights, base_master, momentum):
         rows, width = base_master.shape
+        held = rows * width * (2 * 4 + n * 2)
+        grant = min(GRANT, VMEM - held - 2**20)
         vmem = pl.BlockSpec(memory_space=pltpu.VMEM)
         hbm = pl.BlockSpec(memory_space=pltpu.HBM)
         new_master, new_momentum, all_rows = pl.pallas_call(
@@ -231,7 +235,7 @@
                 pltpu.SemaphoreType.DMA((n, 2, CHUNKS)),
             ],
             compiler_params=pltpu.CompilerParams(
-                collective_id=0, has_side_effects=True, vmem_limit_bytes=16 * 2**20
+                collective_id=0, has_side_effects=True, vmem_limit_bytes=grant
             ),
         )(local_weights, base_master, momentum)
         new_master, new_momentum, all_rows = pl.pallas_call(
@@ -242,7 +246,7 @@
             in_specs=[vmem] * 3,
             out_specs=(hbm,) * 3,
             scratch_shapes=[pltpu.SemaphoreType.DMA((3,))],
-            compiler_params=pltpu.CompilerParams(vmem_limit_bytes=16 * 2**20),
+            compiler_params=pltpu.CompilerParams(vmem_limit_bytes=grant),
         )(*(pltpu.with_memory_space_constraint(x, pltpu.VMEM) for x in (new_master, new_momentum, all_rows)))
         return new_master, new_momentum, all_rows.reshape(n * rows, width)
 

time: 26.4 us -> 23.4 us (0.89)
  local copies, waits for them, and re-layouts: 2.8 us -> 0 us
    unnamed x6 -> x0, local copies, waits for them, and re-layouts: 2.8 us -> none
where the time goes in v3:
time: 23.4 us; the launch traced here: 23.2 us
  Pallas kernels  22.6 us (97%)
  between operations  0.64 us (3%)
    pallas_call x1, Pallas kernels, on_device(): pl.pallas_call(functools.partial(kernel, groups, n), out_shape=(pltpu.VME...  21.4 us
    pallas_call x1, Pallas kernels, on_device(): pl.pallas_call(store, out_shape=tuple((pltpu.HBM(x.shape, x.dtype) for x...  1.16 us

profile of v3, /device:TPU:0, one launch (start us, length us, event | category | flops | bytes accessed | tf_op | source)
XLA Modules:
  0.0 23.2 jit_solution(3767737374936445576)
XLA Ops:
  0.6 21.4 %shard_map.58 = (f32[8,8192]{1,0:T(8,128)S(1)}, f32[8,8192]{1,0:T(8,128)S(1)}, bf16[8,8,8192]{2,1,0:T(8,128)(2,1)S(1)}) custom-call(bf16[1,8,8192]{2,1,0:T(8,128)(2,1)} %weights_in.1, f32[8,8192]{1,0:T(8,128)} %base_in.1, f32[8,8192]{1,0:T(8,128)} %moment_in.1), custom_call_target="tpu_custom_call" | custom-call | tf_op jit(solution)/shard_map/pallas_call | solution.py:216
  22.1 1.2 %shard_map.59 = (f32[8,8192]{1,0:T(8,128)}, f32[8,8192]{1,0:T(8,128)}, bf16[8,8,8192]{2,1,0:T(8,128)(2,1)}) custom-call(f32[8,8192]{1,0:T(8,128)S(1)} %get-tuple-element.9.master, f32[8,8192]{1,0:T(8,128)S(1)} %get-tuple-element.10.moment, bf16[8,8,8192]{2,1,0:T(8,128)(2,1)S(1)} %get-tuple-element.11.rows), custom_call_target="tpu_custom_call" | custom-call | tf_op jit(solution)/shard_map/pallas_call | solution.py:241
